TPU v7x, 32 devices: a whole 2x2x4 slice. The times are simulated.
32 devices in a mesh: tm: 8 (over y, x, core), book: 4 (over z).
Axes of the slice: x: 2, y: 2, z: 4, core: 2. Of those that a mesh axis runs over, the one named last changes fastest.
Arguments:
- q_proj: bfloat16 [16384, 1024], P(('book', 'tm')), parts along dimension 0, may hold values from -52 to 52
- k_proj: bfloat16 [16384, 1024], P(('book', 'tm')), parts along dimension 0, may hold values from -5 to 5
- v_proj: bfloat16 [16384, 1024], P(('book', 'tm')), parts along dimension 0, may hold values from -5 to 5
- gate_bias: float32 [8], replicated, may hold values from -2 to 2
- src_shard: int32 [32, 7], P(('book', 'tm')), parts along dimension 0, may hold values from 0 to 6, as said below
- src_block: int32 [32, 7], P(('book', 'tm')), parts along dimension 0, may hold values from 0 to 3, as said below
- valid: int32 [32, 7], P(('book', 'tm')), parts along dimension 0, may hold values from 0 to 1, as said below
Outputs:
- mixed: bfloat16 [16384, 1024], P(('book', 'tm')), parts along dimension 0
There are 4 independent parts, one for each index of `book`. A program takes and returns all parts, laid end to end along the dimension named above; an argument that names none is the same for every part. Nothing has to cross between parts.
Inputs may be any that keep to these rules, and one draw needn't show every extreme that they name: `src_shard`: in row r the valid entries name distinct segments among r - 7 to r - 1; invalid entries hold 0. `src_block`: invalid entries hold 0. The last segment's list has all 7 entries valid.
All inputs are finite; a program needn't handle non-finite values.
Results may differ from a plain program's by a relative error of at most 0.0033.
Values may be sent and summed in bfloat16 or wider, within the bound.
A program may use at most 64 MiB of HBM per device.

v0:
```python
import functools
import math

import jax
import jax.numpy as jnp
from jax import lax
from jax.experimental import pallas as pl
from jax.experimental.pallas import tpu as pltpu
from jax.sharding import PartitionSpec as P

BLOCK = 128
MASKED = -1e30
FLOOR = -1e29
BARRED = 1e30
UNROLL = 4
GROUPS = ((1, 4), (5, 7))
MESH = pl.DeviceIdType.MESH


def kernel(n, list_len, heads, q_ref, k_ref, v_ref, bias_ref, src_ref, blk_ref, live_ref, out_ref,
           prev_k, prev_v, mem_k, mem_v, send_k, send_v, want_out, want_in,
           top_l, sum_l, acc_l, top_m, sum_m, acc_m,
           relay_k, relay_v, hop_k, hop_v,
           list_ss, list_rs, prev_ss, prev_rs, blk_ss, blk_rs, relay_ss, relay_rs, hop_ss, hop_rs):
    me = lax.axis_index("tm")
    seg, width = q_ref.shape
    hd = width // heads
    per_seg = seg // BLOCK
    far = list_len - 1
    slope = math.log2(math.e) / math.sqrt(hd)

    wants = []
    for d in range(1, list_len + 1):
        want = jnp.int32(-1)
        for e in range(list_len):
            hit = (live_ref[0, e] > 0) & (me - src_ref[0, e] == d)
            want = jnp.where(hit, blk_ref[0, e], want)
        wants.append(want)
        want_out[d - 1] = jnp.full((8, 128), want, jnp.int32)

    def ahead(d):
        return me + d < n

    def behind(d):
        return me - d >= 0

    barrier = pltpu.get_barrier_semaphore()
    for d in range(1, list_len + 1):
        @pl.when(ahead(d))
        def _():
            pl.semaphore_signal(barrier, inc=1, device_id={"tm": me + d}, device_id_type=MESH)

        @pl.when(behind(d))
        def _():
            pl.semaphore_signal(barrier, inc=1, device_id={"tm": me - d}, device_id_type=MESH)
    near = jnp.minimum(me, list_len) + jnp.minimum(n - 1 - me, list_len)
    pl.semaphore_wait(barrier, near)

    detour = n == 8
    odd = lax.rem(me, 2) == 1

    def both(*conditions):
        result = conditions[0]
        for condition in conditions[1:]:
            result = jnp.logical_and(result, condition)
        return result

    def remote(source, target, send, recv, device):
        return pltpu.make_async_remote_copy(source, target, send, recv, device_id={"tm": device},
                                            device_id_type=MESH)

    unfinished = []

    def start(condition, copies):
        @pl.when(condition)
        def _():
            for c in copies():
                c.start()
        unfinished.append((condition, copies))

    def direct(source, d):
        result = both(source >= 0, source + d < n)
        if d == 2:
            result = both(result, lax.rem(source, 2) == 0)
        if detour and d in (3, 4):
            result = both(result, source != 3)
        return result

    def list_copy(d, target, slot=None):
        slot = d - 1 if slot is None else slot
        return [remote(want_out.at[d - 1], want_in.at[slot], list_ss.at[d - 1], list_rs.at[slot], target)]

    def pieces(keys, values):
        half = seg // 2
        return [part.at[pl.ds(i * half, half)] for part in (keys, values) for i in range(2)]

    def prev_copies(keys, values, target, chosen=range(4)):
        return [remote(pieces(keys, values)[i], pieces(prev_k, prev_v)[i], prev_ss.at[i], prev_rs.at[i], target)
                for i in chosen]

    def relay_copies(chosen=range(4)):
        return [remote(pieces(k_ref, v_ref)[i], pieces(relay_k, relay_v)[i], relay_ss.at[i], relay_rs.at[i], 7)
                for i in chosen]

    def block_copies(d, target, slot=None):
        slot = d - 2 if slot is None else slot
        return [remote(here.at[slot], there.at[d - 1], blk_ss.at[i, slot], blk_rs.at[i, d - 2], target)
                for i, (here, there) in enumerate(((send_k, mem_k), (send_v, mem_v)))]

    def hop_in(d):
        return [remote(here.at[d - 2], there, blk_ss.at[i, d - 2], hop_rs.at[i], d - 2)
                for i, (here, there) in enumerate(((send_k, hop_k), (send_v, hop_v)))]

    def hop_out(d):
        return [remote(here, there.at[d - 1], hop_ss.at[i], blk_rs.at[i, d - 2], d)
                for i, (here, there) in enumerate(((hop_k, mem_k), (hop_v, mem_v)))]

    def pick(want, from_k, from_v, to_k, to_v):
        ones = [jnp.where(want == b, 1.0, 0.0)[:1].astype(jnp.bfloat16) for b in range(per_seg)]

        def one_strip(h, carry):
            cols = pl.ds(pl.multiple_of(h * 128, 128), 128)
            for source, target in ((from_k, to_k), (from_v, to_v)):
                total = source[:BLOCK, cols] * ones[0]
                for b in range(1, per_seg):
                    total = total + source[b * BLOCK:(b + 1) * BLOCK, cols] * ones[b]
                target[:, cols] = total
            return carry

        lax.fori_loop(0, width // 128, one_strip, 0)

    for d in range(list_len, 1, -1):
        start(direct(me - d, d), lambda d=d: list_copy(d, me - d))
    start(both(odd, behind(2)), lambda: list_copy(2, me - 1, list_len))
    if detour:
        start(me == 6, lambda: list_copy(3, 7))
        start(me == 3, relay_copies)
        start(both(ahead(1), me != 3), lambda: prev_copies(k_ref, v_ref, me + 1))
    else:
        start(ahead(1), lambda: prev_copies(k_ref, v_ref, me + 1))

    for d in range(list_len, 1, -1):
        @pl.when(direct(me, d))
        def _():
            for c in list_copy(d, me + d):
                c.wait_recv()
            pick(want_in[d - 1], k_ref, v_ref, send_k.at[d - 2], send_v.at[d - 2])
    for d in range(list_len, 1, -1):
        if detour and d in (6, 7):
            start(me == 0, lambda d=d: hop_in(d))
            start(both(direct(me, d), me != 0), lambda d=d: block_copies(d, me + d))
        else:
            start(direct(me, d), lambda d=d: block_copies(d, me + d))

    def absorb(load_k, load_v, top, total, acc, some_wants=None, causal=False, first=False):
        lives = None if some_wants is None else [jnp.full((1, seg), w, jnp.int32) >= 0 for w in some_wants]

        def one_head(h, carry):
            cols = pl.ds(pl.multiple_of(h * hd, hd), hd)
            row = pl.ds(h, 1)
            s = lax.dot_general(load_k(cols), q_ref[:, cols], (((1,), (1,)), ((), ())),
                                preferred_element_type=jnp.float32)
            if causal:
                key_at = lax.broadcasted_iota(jnp.int32, s.shape, 0)
                query_at = lax.broadcasted_iota(jnp.int32, s.shape, 1)
                s = jnp.where(key_at <= query_at, s, MASKED)
            new = None if first else top[row, :]
            if lives is None:
                high = jnp.max(s, axis=0, keepdims=True)
                new = high if first else jnp.maximum(new, high)
                p = jnp.exp2((s - new) * slope)
            else:
                strips = [s[i * BLOCK:(i + 1) * BLOCK] for i in range(len(lives))]
                for strip, live in zip(strips, lives):
                    high = jnp.where(live, jnp.max(strip, axis=0, keepdims=True), FLOOR)
                    new = high if new is None else jnp.maximum(new, high)
                p = jnp.concatenate([jnp.exp2((strip - jnp.where(live, new, BARRED)) * slope)
                                     for strip, live in zip(strips, lives)], axis=0)
            part = jnp.sum(p, axis=0, keepdims=True)
            mixed = lax.dot_general(load_v(cols), p.astype(jnp.bfloat16), (((0,), (0,)), ((), ())),
                                    preferred_element_type=jnp.float32)
            if first:
                total[row, :] = part
                acc[cols, :] = mixed
            else:
                shrink = jnp.exp2((top[row, :] - new) * slope)
                total[row, :] = total[row, :] * shrink + part
                acc[cols, :] = acc[cols, :] * shrink + mixed
            top[row, :] = new
            return carry

        lax.fori_loop(0, heads, one_head, 0, unroll=UNROLL)

    @pl.when(jnp.logical_not(behind(1)))
    def _():
        sum_m[...] = jnp.zeros_like(sum_m)
        acc_m[...] = jnp.zeros_like(acc_m)
    for d in range(2, list_len + 1):
        @pl.when(jnp.logical_not(behind(d)))
        def _():
            mem_k[d - 1] = jnp.zeros((BLOCK, width), jnp.bfloat16)
            mem_v[d - 1] = jnp.zeros((BLOCK, width), jnp.bfloat16)

    absorb(lambda c: k_ref[:, c], lambda c: v_ref[:, c], top_l, sum_l, acc_l, causal=True, first=True)

    if detour:
        for d in (6, 7):
            @pl.when(me == d - 2)
            def _():
                for c in hop_in(d):
                    c.wait_recv()
            start(me == d - 2, lambda d=d: hop_out(d))

        def forward(i):
            @pl.when(me == 7)
            def _():
                relay_copies([i])[0].wait_recv()
            start(me == 7, lambda: prev_copies(relay_k, relay_v, 4, [i]))

        forward(0)

    def take_prev():
        for c in prev_copies(k_ref, v_ref, me - 1):
            c.wait_recv()

    pl.when(behind(1))(take_prev)
    pass_on = both(jnp.logical_not(odd), behind(1), ahead(1))

    @pl.when(pass_on)
    def _():
        list_copy(2, me, list_len)[0].wait_recv()
        pick(want_in[list_len], prev_k, prev_v, send_k.at[far], send_v.at[far])
    start(pass_on, lambda: block_copies(2, me + 1, far))

    @pl.when(behind(1))
    def _():
        absorb(lambda c: prev_k[:, c], lambda c: prev_v[:, c], top_l, sum_l, acc_l)
        pick(want_out[0], prev_k, prev_v, mem_k.at[0], mem_v.at[0])

    if detour:
        for i in range(1, 4):
            forward(i)

        @pl.when(me == 7)
        def _():
            list_copy(3, 6)[0].wait_recv()
            pick(want_in[2], relay_k, relay_v, send_k.at[1], send_v.at[1])
            pick(want_out[3], relay_k, relay_v, mem_k.at[3], mem_v.at[3])
        start(me == 7, lambda: block_copies(3, 6))

    for low, high in GROUPS:
        for d in range(max(low, 2), min(high, list_len) + 1):
            @pl.when(both(behind(d), me != 7) if detour and d == 4 else behind(d))
            def _():
                for c in block_copies(d, me - d):
                    c.wait_recv()

        @pl.when(behind(low))
        def _():
            last = min(high, list_len)

            def load(blocks):
                return lambda c: blocks[low - 1:last, :, c].reshape((last - low + 1) * BLOCK, hd)
            absorb(load(mem_k), load(mem_v), top_m, sum_m, acc_m, some_wants=wants[low - 1:last], first=low == 1)

    def finish(h, carry):
        cols = pl.ds(pl.multiple_of(h * hd, hd), hd)
        row = pl.ds(h, 1)
        gate = 1.0 / (1.0 + jnp.exp(jnp.full((1, seg), -bias_ref[h], jnp.float32)))
        mixed = (acc_m[cols, :] * (gate / jnp.maximum(sum_m[row, :], 1.0))
                 + acc_l[cols, :] * ((1.0 - gate) / jnp.maximum(sum_l[row, :], 1.0)))
        out_ref[:, cols] = mixed.T.astype(jnp.bfloat16)
        return carry

    lax.fori_loop(0, heads, finish, 0, unroll=UNROLL)

    for condition, copies in unfinished:
        @pl.when(condition)
        def _():
            for c in copies():
                c.wait_send()


def shards(n, q_proj, k_proj, v_proj, gate_bias, src_shard, src_block, valid):
    seg, width = q_proj.shape
    heads = gate_bias.shape[0]
    list_len = src_shard.shape[1]
    far = list_len - 1
    vmem = pl.BlockSpec(memory_space=pltpu.VMEM)
    smem = pl.BlockSpec(memory_space=pltpu.SMEM)
    return pl.pallas_call(
        functools.partial(kernel, n, list_len, heads),
        out_shape=jax.ShapeDtypeStruct((seg, width), jnp.bfloat16),
        in_specs=[vmem] * 3 + [smem] * 4,
        out_specs=vmem,
        scratch_shapes=[
            pltpu.VMEM((seg, width), jnp.bfloat16),
            pltpu.VMEM((seg, width), jnp.bfloat16),
            pltpu.VMEM((list_len, BLOCK, width), jnp.bfloat16),
            pltpu.VMEM((list_len, BLOCK, width), jnp.bfloat16),
            pltpu.VMEM((far + 1, BLOCK, width), jnp.bfloat16),
            pltpu.VMEM((far + 1, BLOCK, width), jnp.bfloat16),
            pltpu.VMEM((list_len, 8, 128), jnp.int32),
            pltpu.VMEM((list_len + 1, 8, 128), jnp.int32),
            pltpu.VMEM((heads, seg), jnp.float32),
            pltpu.VMEM((heads, seg), jnp.float32),
            pltpu.VMEM((width, seg), jnp.float32),
            pltpu.VMEM((heads, seg), jnp.float32),
            pltpu.VMEM((heads, seg), jnp.float32),
            pltpu.VMEM((width, seg), jnp.float32),
            pltpu.VMEM((seg, width), jnp.bfloat16),
            pltpu.VMEM((seg, width), jnp.bfloat16),
            pltpu.VMEM((BLOCK, width), jnp.bfloat16),
            pltpu.VMEM((BLOCK, width), jnp.bfloat16),
            pltpu.SemaphoreType.DMA((list_len,)),
            pltpu.SemaphoreType.DMA((list_len + 1,)),
            pltpu.SemaphoreType.DMA((4,)),
            pltpu.SemaphoreType.DMA((4,)),
            pltpu.SemaphoreType.DMA((2, far + 1)),
            pltpu.SemaphoreType.DMA((2, far)),
            pltpu.SemaphoreType.DMA((4,)),
            pltpu.SemaphoreType.DMA((4,)),
            pltpu.SemaphoreType.DMA((2,)),
            pltpu.SemaphoreType.DMA((2,)),
        ],
        compiler_params=pltpu.CompilerParams(collective_id=0, has_side_effects=True),
    )(q_proj, k_proj, v_proj, gate_bias, src_shard, src_block, valid)


def solution(mesh):
    rows = P(("book", "tm"), None)
    return jax.shard_map(functools.partial(shards, mesh.shape["tm"]), mesh=mesh,
                         in_specs=(rows, rows, rows, P(), rows, rows, rows), out_specs=rows, check_vma=False)
```

profile of v0, /device:TPU:28, one launch (start us, length us, event | category | flops | bytes accessed | tf_op | source)
XLA Modules:
  0.0 63.9 jit_solution(1909260613037388593)
XLA Ops:
  0.0 61.6 %shard_map.73 = bf16[512,1024]{1,0:T(8,128)(2,1)} custom-call(bf16[512,1024]{1,0:T(8,128)(2,1)} %q_ref.1, bf16[512,1024]{1,0:T(8,128)(2,1)} %k_ref.1, bf16[512,1024]{1,0:T(8,128)(2,1)} %v_ref.1, f32[8]{0:T(128)} %bias_ref.1, s32[1,7]{1,0:T(1,128)} %src_ref.1, s32[1,7]{1,0:T(1,128)} %blk_ref.1, s32[1,7]{1,0:T(1,128)} %live_ref.1), custom_call_target="tpu_custom_call" | custom-call | tf_op jit(solution)/shard_map/pallas_call | solution.py:291
  61.6 2.3 %copy.9 = bf16[512,1024]{1,0:T(8,128)(2,1)} copy(bf16[512,1024]{1,0:T(8,128)(2,1)} %shard_map.73) | data formatting | bytes 2097152
where the time goes:
time: 64 us; the launch traced here: 63.9 us
  Pallas kernels  61.6 us (96%)
  local copies, waits for them, and re-layouts  2.26 us (4%)
    pallas_call x1, Pallas kernels, shards(): pl.pallas_call(functools.partial(kernel, n, list_len, heads), out_shape=j...  61.6 us
    unnamed x1, local copies, waits for them, and re-layouts  2.26 us

commit v1 on v0

--- a/solution.py
+++ b/solution.py
@@ -281,7 +281,340 @@
                 c.wait_send()
 
 
-def shards(n, q_proj, k_proj, v_proj, gate_bias, src_shard, src_block, valid):
+ORDER = ((0, 0, 0, 0, 0, 0, 0),
+         (1, 0, 0, 0, 0, 0, 0),
+         (1, 0, 0, 0, 0, 0, 2),
+         (1, 2, 0, 0, 0, 0, 3),
+         (4, 1, 0, 0, 0, 3, 2),
+         (1, 5, 2, 0, 0, 3, 4),
+         (1, 3, 2, 4, 0, 6, 5),
+         (1, 4, 2, 3, 5, 6, 7))
+STAGES = ((0, 3), (3, 2), (5, 1), (6, 1))
+HOLDERS = ((), (), (0,), (0, 2), (1, 2), (1, 2, 4), (1, 2, 4, 7), (1, 2, 4, 6))
+SENDS = {0: ((2, 2, "own"), (3, 3, "own")),
+         1: ((7, 6, "own"), (6, 5, "own"), (4, 3, "own"), (5, 4, "own")),
+         2: ((5, 3, "own"), (4, 2, "own"), (6, 4, "own"), (7, 5, "own"), (3, 2, "prev")),
+         4: ((6, 2, "own"), (7, 3, "own"), (6, 6, "aux"), (7, 7, "aux"), (5, 5, "aux"), (5, 2, "prev")),
+         6: ((7, 2, "prev"),),
+         7: ((6, 3, "aux"),)}
+SLOTS = 6
+VMEM_LIMIT = 60 * 2 ** 20
+
+
+def eight(list_len, heads, q_hbm, k_hbm, v_hbm, bias_hbm, src_hbm, blk_hbm, live_hbm, out_ref,
+          q_ref, k_ref, v_ref, bias_ref, src_ref, blk_ref, live_ref, load_s, prev_k, prev_v, aux_k, aux_v, mem_k, mem_v, send_k, send_v, want_out, want_in,
+          top_l, sum_l, acc_l, top_m, sum_m, acc_m,
+          list_ss, list_rs, prev_ss, prev_rs, aux_ss, aux_rs, blk_ss, blk_rs):
+    me = lax.axis_index("tm")
+    seg, width = q_ref.shape
+    hd = width // heads
+    per_seg = seg // BLOCK
+    loads = [pltpu.make_async_copy(source, target, load_s.at[i]) for i, (source, target) in enumerate(
+        ((src_hbm, src_ref), (blk_hbm, blk_ref), (live_hbm, live_ref), (bias_hbm, bias_ref),
+         (k_hbm, k_ref), (q_hbm, q_ref), (v_hbm, v_ref)))]
+    for load in loads:
+        load.start()
+    barrier = pltpu.get_barrier_semaphore()
+    for other in range(8):
+        @pl.when(me != other)
+        def _():
+            pl.semaphore_signal(barrier, inc=1, device_id={"tm": other}, device_id_type=MESH)
+    places = len(ORDER[0])
+    slope = math.log2(math.e) / math.sqrt(hd)
+
+    def any_of(devices):
+        result = me == devices[0]
+        for device in devices[1:]:
+            result = jnp.logical_or(result, me == device)
+        return result
+
+    def want_of(distance):
+        want = jnp.int32(-1)
+        for e in range(list_len):
+            hit = (live_ref[0, e] > 0) & (me - src_ref[0, e] == distance)
+            want = jnp.where(hit, blk_ref[0, e], want)
+        return want
+
+    for load in loads[:3]:
+        load.wait()
+    wants = []
+    for p in range(places):
+        distance = jnp.int32(100)
+        for r in range(8):
+            if ORDER[r][p]:
+                distance = jnp.where(me == r, ORDER[r][p], distance)
+        wants.append(want_of(distance))
+    row = lax.broadcasted_iota(jnp.int32, (8, 128), 0)
+    tile = jnp.full((8, 128), -1, jnp.int32)
+    for d in range(1, list_len + 1):
+        tile = jnp.where(row == d - 1, want_of(d), tile)
+    want_out[...] = tile
+    pl.semaphore_wait(barrier, 7)
+
+    def remote(source, target, send, recv, device):
+        return pltpu.make_async_remote_copy(source, target, send, recv, device_id={"tm": device},
+                                            device_id_type=MESH)
+
+    def pieces(keys, values):
+        half = width // 2
+        return [part.at[:, pl.ds(i * half, half)] for i in range(2) for part in (keys, values)]
+
+    def prev_copy(i, keys, values, device):
+        return remote(pieces(keys, values)[i], pieces(prev_k, prev_v)[i], prev_ss.at[i], prev_rs.at[i], device)
+
+    def aux_copy(i, device):
+        return remote(pieces(k_hbm, v_hbm)[i], pieces(aux_k, aux_v)[i], aux_ss.at[i], aux_rs.at[i], device)
+
+    def list_copy(i, slot, device):
+        return remote(want_out, want_in.at[slot], list_ss.at[i], list_rs.at[slot], device)
+
+    def block_copies(slot, place, device):
+        return [remote(here.at[slot], there.at[place], blk_ss.at[i, slot], blk_rs.at[i, place], device)
+                for i, (here, there) in enumerate(((send_k, mem_k), (send_v, mem_v)))]
+
+    def pick(want, source, to_k, to_v):
+        from_k, from_v = {"own": (k_ref, v_ref), "prev": (prev_k, prev_v), "aux": (aux_k, aux_v)}[source]
+        ones = [jnp.where(want == b, 1.0, 0.0).astype(jnp.bfloat16) for b in range(per_seg)]
+
+        def one_strip(h, carry):
+            cols = pl.ds(pl.multiple_of(h * 128, 128), 128)
+            for origin, target in ((from_k, to_k), (from_v, to_v)):
+                total = origin[:BLOCK, cols] * ones[0]
+                for b in range(1, per_seg):
+                    total = total + origin[b * BLOCK:(b + 1) * BLOCK, cols] * ones[b]
+                target[:, cols] = total
+            return carry
+
+        lax.fori_loop(0, width // 128, one_strip, 0)
+
+    def pick_send(device, chosen):
+        for slot in chosen:
+            reader, distance, source = SENDS[device][slot]
+            pick(want_in[reader - 2, distance - 1:distance, :], source, send_k.at[slot], send_v.at[slot])
+
+    def start_send(device, chosen):
+        for slot in chosen:
+            reader, distance, source = SENDS[device][slot]
+            for c in block_copies(slot, ORDER[reader].index(distance), reader):
+                c.start()
+
+    def pick_own(place, source):
+        pick(jnp.full((1, 128), wants[place], jnp.int32), source, mem_k.at[place], mem_v.at[place])
+
+    @pl.when(me == 3)
+    def _():
+        for i in range(4):
+            aux_copy(i, 7).start()
+
+    @pl.when(me == 0)
+    def _():
+        for i in range(4):
+            aux_copy(i, 4).start()
+    for r in range(2, 8):
+        @pl.when(me == r)
+        def _():
+            for i, holder in enumerate(HOLDERS[r]):
+                list_copy(i, r - 2, holder).start()
+    gives = any_of((0, 1, 2, 4, 5, 6))
+
+    @pl.when(gives)
+    def _():
+        for i in range(4):
+            prev_copy(i, k_hbm, v_hbm, me + 1).start()
+
+    for load in loads[3:]:
+        load.wait()
+
+    for device in (0, 1, 2, 4, 6, 7):
+        @pl.when(me == device)
+        def _():
+            for r in range(2, 8):
+                if device in HOLDERS[r]:
+                    list_copy(0, r - 2, r).wait_recv()
+            pick_send(device, [i for i, entry in enumerate(SENDS[device]) if entry[2] == "own"])
+            if device == 1:
+                start_send(1, (0, 1))
+
+    for devices, place in (((1, 2), 1), ((1, 2, 3, 4), 2), ((6,), 4)):
+        @pl.when(any_of(devices))
+        def _():
+            mem_k[place] = jnp.zeros((BLOCK, width), jnp.bfloat16)
+            mem_v[place] = jnp.zeros((BLOCK, width), jnp.bfloat16)
+
+    def absorb(load_k, load_v, top, total, acc, some_wants=None, causal=False, first=False):
+        lives = None if some_wants is None else [jnp.full((1, seg), w, jnp.int32) >= 0 for w in some_wants]
+
+        def one_head(h, carry):
+            cols = pl.ds(pl.multiple_of(h * hd, hd), hd)
+            row = pl.ds(h, 1)
+            s = lax.dot_general(load_k(cols), q_ref[:, cols], (((1,), (1,)), ((), ())),
+                                preferred_element_type=jnp.float32)
+            if causal:
+                key_at = lax.broadcasted_iota(jnp.int32, s.shape, 0)
+                query_at = lax.broadcasted_iota(jnp.int32, s.shape, 1)
+                s = jnp.where(key_at <= query_at, s, MASKED)
+            new = None if first else top[row, :]
+            if lives is None:
+                high = jnp.max(s, axis=0, keepdims=True)
+                new = high if first else jnp.maximum(new, high)
+                p = jnp.exp2((s - new) * slope)
+            else:
+                strips = [s[i * BLOCK:(i + 1) * BLOCK] for i in range(len(lives))]
+                for strip, live in zip(strips, lives):
+                    high = jnp.where(live, jnp.max(strip, axis=0, keepdims=True), FLOOR)
+                    new = high if new is None else jnp.maximum(new, high)
+                p = jnp.concatenate([jnp.exp2((strip - jnp.where(live, new, BARRED)) * slope)
+                                     for strip, live in zip(strips, lives)], axis=0)
+            part = jnp.sum(p, axis=0, keepdims=True)
+            mixed = lax.dot_general(load_v(cols), p.astype(jnp.bfloat16), (((0,), (0,)), ((), ())),
+                                    preferred_element_type=jnp.float32)
+            if first:
+                total[row, :] = part
+                acc[cols, :] = mixed
+            else:
+                shrink = jnp.exp2((top[row, :] - new) * slope)
+                total[row, :] = total[row, :] * shrink + part
+                acc[cols, :] = acc[cols, :] * shrink + mixed
+            top[row, :] = new
+            return carry
+
+        lax.fori_loop(0, heads, one_head, 0, unroll=UNROLL)
+
+    @pl.when(me == 0)
+    def _():
+        sum_m[...] = jnp.zeros_like(sum_m)
+        acc_m[...] = jnp.zeros_like(acc_m)
+
+    absorb(lambda c: k_ref[:, c], lambda c: v_ref[:, c], top_l, sum_l, acc_l, causal=True, first=True)
+
+    def forward(i):
+        @pl.when(me == 7)
+        def _():
+            aux_copy(i, 3).wait_recv()
+            prev_copy(i, aux_k, aux_v, 4).start()
+
+    def take_prev(chosen):
+        for i in chosen:
+            prev_copy(i, k_hbm, v_hbm, 0).wait_recv()
+
+    def take_aux(chosen):
+        for i in chosen:
+            aux_copy(i, 0).wait_recv()
+
+    forward(0)
+
+    @pl.when(me == 0)
+    def _():
+        for i in range(4):
+            aux_copy(i, 4).wait_send()
+        start_send(0, (0, 1))
+
+    @pl.when(me == 2)
+    def _():
+        take_prev(range(4))
+        start_send(2, (0, 1, 2, 3))
+
+    @pl.when(me == 4)
+    def _():
+        take_aux(range(4))
+        start_send(4, (0, 1))
+        pick_send(4, (2, 3, 4))
+        start_send(4, (2, 3, 4))
+        pick_own(0, "aux")
+
+    @pl.when(me == 2)
+    def _():
+        pick_send(2, [4])
+        start_send(2, [4])
+
+    @pl.when(any_of((1, 3, 4, 5, 6, 7)))
+    def _():
+        take_prev(range(4))
+
+    @pl.when(me == 4)
+    def _():
+        pick_send(4, [5])
+        start_send(4, [5])
+        pick_own(1, "prev")
+
+    @pl.when(me == 6)
+    def _():
+        pick_send(6, [0])
+        start_send(6, [0])
+
+    @pl.when(any_of((1, 2, 3, 5, 6, 7)))
+    def _():
+        pick_own(0, "prev")
+
+    @pl.when(me >= 1)
+    def _():
+        absorb(lambda c: prev_k[:, c], lambda c: prev_v[:, c], top_l, sum_l, acc_l)
+
+    @pl.when(me == 1)
+    def _():
+        for i in range(4):
+            prev_copy(i, k_hbm, v_hbm, 2).wait_send()
+        start_send(1, (2, 3))
+
+    for i in range(1, 4):
+        forward(i)
+
+    @pl.when(me == 7)
+    def _():
+        pick_send(7, [0])
+        start_send(7, [0])
+        pick_own(1, "aux")
+
+    remote_places = {r: [] for r in range(8)}
+    for device, entries in SENDS.items():
+        for reader, distance, source in entries:
+            remote_places[reader].append(ORDER[reader].index(distance))
+
+    for low, count in STAGES:
+        for place in range(low, low + count):
+            readers = [r for r in range(8) if place in remote_places[r]]
+            if readers:
+                @pl.when(any_of(readers))
+                def _():
+                    for c in block_copies(0, place, 0):
+                        c.wait_recv()
+        users = [r for r in range(8) if any(ORDER[r][low:low + count])]
+
+        @pl.when(any_of(users))
+        def _():
+            def load(blocks):
+                return lambda c: blocks[low:low + count, :, c].reshape(count * BLOCK, hd)
+            absorb(load(mem_k), load(mem_v), top_m, sum_m, acc_m, some_wants=wants[low:low + count],
+                   first=low == 0)
+
+    def finish(h, carry):
+        cols = pl.ds(pl.multiple_of(h * hd, hd), hd)
+        row = pl.ds(h, 1)
+        gate = 1.0 / (1.0 + jnp.exp(jnp.full((1, seg), -bias_ref[h], jnp.float32)))
+        mixed = (acc_m[cols, :] * (gate / jnp.maximum(sum_m[row, :], 1.0))
+                 + acc_l[cols, :] * ((1.0 - gate) / jnp.maximum(sum_l[row, :], 1.0)))
+        out_ref[:, cols] = mixed.T.astype(jnp.bfloat16)
+        return carry
+
+    lax.fori_loop(0, heads, finish, 0, unroll=UNROLL)
+
+    for device in range(8):
+        @pl.when(me == device)
+        def _():
+            for i in range(len(HOLDERS[device])):
+                list_copy(i, 0, 0).wait_send()
+            for slot in range(len(SENDS.get(device, ()))):
+                for c in block_copies(slot, 0, 0):
+                    c.wait_send()
+            if device == 3:
+                for i in range(4):
+                    aux_copy(i, 4).wait_send()
+            if device not in (1, 3):
+                for i in range(4):
+                    prev_copy(i, k_hbm, v_hbm, 2).wait_send()
+
+
+def general(n, q_proj, k_proj, v_proj, gate_bias, src_shard, src_block, valid):
     seg, width = q_proj.shape
     heads = gate_bias.shape[0]
     list_len = src_shard.shape[1]
@@ -327,6 +660,34 @@
     )(q_proj, k_proj, v_proj, gate_bias, src_shard, src_block, valid)
 
 
+def shards(n, q_proj, k_proj, v_proj, gate_bias, src_shard, src_block, valid):
+    seg, width = q_proj.shape
+    heads = gate_bias.shape[0]
+    list_len = src_shard.shape[1]
+    vmem = pl.BlockSpec(memory_space=pltpu.VMEM)
+    if n != 8:
+        return general(n, q_proj, k_proj, v_proj, gate_bias, src_shard, src_block, valid)
+    whole = pltpu.VMEM((seg, width), jnp.bfloat16)
+    return pl.pallas_call(
+        functools.partial(eight, list_len, heads),
+        out_shape=jax.ShapeDtypeStruct((seg, width), jnp.bfloat16),
+        in_specs=[pl.BlockSpec(memory_space=pltpu.HBM)] * 7,
+        out_specs=vmem,
+        scratch_shapes=[whole] * 3 + [pltpu.SMEM(gate_bias.shape, jnp.float32)]
+        + [pltpu.SMEM(src_shard.shape, jnp.int32)] * 3 + [pltpu.SemaphoreType.DMA((7,))] + [whole] * 4
+        + [pltpu.VMEM((len(ORDER[0]), BLOCK, width), jnp.bfloat16)] * 2
+        + [pltpu.VMEM((SLOTS, BLOCK, width), jnp.bfloat16)] * 2
+        + [pltpu.VMEM((8, 128), jnp.int32), pltpu.VMEM((6, 8, 128), jnp.int32)]
+        + [pltpu.VMEM((heads, seg), jnp.float32), pltpu.VMEM((heads, seg), jnp.float32),
+           pltpu.VMEM((width, seg), jnp.float32)] * 2
+        + [pltpu.SemaphoreType.DMA((4,)), pltpu.SemaphoreType.DMA((6,))]
+        + [pltpu.SemaphoreType.DMA((4,))] * 4
+        + [pltpu.SemaphoreType.DMA((2, SLOTS)), pltpu.SemaphoreType.DMA((2, len(ORDER[0])))],
+        compiler_params=pltpu.CompilerParams(collective_id=0, has_side_effects=True,
+                                             vmem_limit_bytes=VMEM_LIMIT),
+    )(q_proj, k_proj, v_proj, gate_bias, src_shard, src_block, valid)
+
+
 def solution(mesh):
     rows = P(("book", "tm"), None)
     return jax.shard_map(functools.partial(shards, mesh.shape["tm"]), mesh=mesh,

time: 64 us -> 61.8 us (0.966)
  the two profiles are of different devices: /device:TPU:28 before, /device:TPU:15 now
where the time goes in v1:
time: 61.8 us; the launch traced here: 61.6 us
  Pallas kernels  59.3 us (96%)
  local copies, waits for them, and re-layouts  2.26 us (4%)
    pallas_call x1, Pallas kernels, shards(): pl.pallas_call(functools.partial(eight, list_len, heads), out_shape=jax.S...  59.3 us
    unnamed x1, local copies, waits for them, and re-layouts  2.26 us

profile of v1, /device:TPU:15, one launch (start us, length us, event | category | flops | bytes accessed | tf_op | source)
XLA Modules:
  0.0 61.6 jit_solution(5173525772814254355)
XLA Ops:
  0.0 59.3 %shard_map.73 = bf16[512,1024]{1,0:T(8,128)(2,1)} custom-call(bf16[512,1024]{1,0:T(8,128)(2,1)} %q_hbm.1, bf16[512,1024]{1,0:T(8,128)(2,1)} %k_hbm.1, bf16[512,1024]{1,0:T(8,128)(2,1)} %v_hbm.1, f32[8]{0:T(128)} %bias_hbm.1, s32[1,7]{1,0:T(1,128)} %src_hbm.1, s32[1,7]{1,0:T(1,128)} %blk_hbm.1, s32[1,7]{1,0:T(1,128)} %live_hbm.1), custom_call_target="tpu_custom_call" | custom-call | tf_op jit(solution)/shard_map/pallas_call | solution.py:671
  59.4 2.3 %copy.9 = bf16[512,1024]{1,0:T(8,128)(2,1)} copy(bf16[512,1024]{1,0:T(8,128)(2,1)} %shard_map.73) | data formatting | bytes 2097152

commit v2 on v1

--- a/solution.py
+++ b/solution.py
@@ -285,15 +285,15 @@
          (1, 0, 0, 0, 0, 0, 0),
          (1, 0, 0, 0, 0, 0, 2),
          (1, 2, 0, 0, 0, 0, 3),
-         (4, 1, 0, 0, 0, 3, 2),
+         (4, 1, 0, 0, 0, 2, 3),
          (1, 5, 2, 0, 0, 3, 4),
-         (1, 3, 2, 4, 0, 6, 5),
-         (1, 4, 2, 3, 5, 6, 7))
+         (1, 3, 2, 5, 0, 6, 4),
+         (1, 4, 2, 3, 6, 5, 7))
 STAGES = ((0, 3), (3, 2), (5, 1), (6, 1))
 HOLDERS = ((), (), (0,), (0, 2), (1, 2), (1, 2, 4), (1, 2, 4, 7), (1, 2, 4, 6))
 SENDS = {0: ((2, 2, "own"), (3, 3, "own")),
          1: ((7, 6, "own"), (6, 5, "own"), (4, 3, "own"), (5, 4, "own")),
-         2: ((5, 3, "own"), (4, 2, "own"), (6, 4, "own"), (7, 5, "own"), (3, 2, "prev")),
+         2: ((5, 3, "own"), (4, 2, "own"), (7, 5, "own"), (6, 4, "own"), (3, 2, "prev")),
          4: ((6, 2, "own"), (7, 3, "own"), (6, 6, "aux"), (7, 7, "aux"), (5, 5, "aux"), (5, 2, "prev")),
          6: ((7, 2, "prev"),),
          7: ((6, 3, "aux"),)}
@@ -304,7 +304,7 @@
 def eight(list_len, heads, q_hbm, k_hbm, v_hbm, bias_hbm, src_hbm, blk_hbm, live_hbm, out_ref,
           q_ref, k_ref, v_ref, bias_ref, src_ref, blk_ref, live_ref, load_s, prev_k, prev_v, aux_k, aux_v, mem_k, mem_v, send_k, send_v, want_out, want_in,
           top_l, sum_l, acc_l, top_m, sum_m, acc_m,
-          list_ss, list_rs, prev_ss, prev_rs, aux_ss, aux_rs, blk_ss, blk_rs):
+          list_ss, list_rs, prev_ss, prev_rs, aux_ss, aux_rs, blk_ss, blk_rs, turn):
     me = lax.axis_index("tm")
     seg, width = q_ref.shape
     hd = width // heads
@@ -503,12 +503,6 @@
 
     forward(0)
 
-    @pl.when(me == 0)
-    def _():
-        for i in range(4):
-            aux_copy(i, 4).wait_send()
-        start_send(0, (0, 1))
-
     @pl.when(me == 2)
     def _():
         take_prev(range(4))
@@ -516,8 +510,9 @@
 
     @pl.when(me == 4)
     def _():
-        take_aux(range(4))
+        take_aux(range(3))
         start_send(4, (0, 1))
+        take_aux([3])
         pick_send(4, (2, 3, 4))
         start_send(4, (2, 3, 4))
         pick_own(0, "aux")
@@ -555,6 +550,15 @@
         for i in range(4):
             prev_copy(i, k_hbm, v_hbm, 2).wait_send()
         start_send(1, (2, 3))
+        for slot in (0, 1):
+            for c in block_copies(slot, 0, 2):
+                c.wait_send()
+        pl.semaphore_signal(turn, inc=1, device_id={"tm": 0}, device_id_type=MESH)
+
+    @pl.when(me == 0)
+    def _():
+        pl.semaphore_wait(turn, 1)
+        start_send(0, (0, 1))
 
     for i in range(1, 4):
         forward(i)
@@ -603,10 +607,10 @@
         def _():
             for i in range(len(HOLDERS[device])):
                 list_copy(i, 0, 0).wait_send()
-            for slot in range(len(SENDS.get(device, ()))):
+            for slot in range(2 if device == 1 else 0, len(SENDS.get(device, ()))):
                 for c in block_copies(slot, 0, 0):
                     c.wait_send()
-            if device == 3:
+            if device in (0, 3):
                 for i in range(4):
                     aux_copy(i, 4).wait_send()
             if device not in (1, 3):
@@ -682,7 +686,8 @@
            pltpu.VMEM((width, seg), jnp.float32)] * 2
         + [pltpu.SemaphoreType.DMA((4,)), pltpu.SemaphoreType.DMA((6,))]
         + [pltpu.SemaphoreType.DMA((4,))] * 4
-        + [pltpu.SemaphoreType.DMA((2, SLOTS)), pltpu.SemaphoreType.DMA((2, len(ORDER[0])))],
+        + [pltpu.SemaphoreType.DMA((2, SLOTS)), pltpu.SemaphoreType.DMA((2, len(ORDER[0]))),
+           pltpu.SemaphoreType.REGULAR],
         compiler_params=pltpu.CompilerParams(collective_id=0, has_side_effects=True,
                                              vmem_limit_bytes=VMEM_LIMIT),
     )(q_proj, k_proj, v_proj, gate_bias, src_shard, src_block, valid)

time: 61.8 us -> 57.4 us (0.929)
  the two profiles are of different devices: /device:TPU:15 before, /device:TPU:27 now
where the time goes in v2:
time: 57.4 us; the launch traced here: 57.2 us
  Pallas kernels  55 us (96%)
  local copies, waits for them, and re-layouts  2.26 us (4%)
    pallas_call x1, Pallas kernels, shards(): pl.pallas_call(functools.partial(eight, list_len, heads), out_shape=jax.S...  55 us
    unnamed x1, local copies, waits for them, and re-layouts  2.26 us

profile of v2, /device:TPU:27, one launch (start us, length us, event | category | flops | bytes accessed | tf_op | source)
XLA Modules:
  0.0 57.2 jit_solution(1995813726971049634)
XLA Ops:
  0.0 55.0 %shard_map.73 = bf16[512,1024]{1,0:T(8,128)(2,1)} custom-call(bf16[512,1024]{1,0:T(8,128)(2,1)} %q_hbm.1, bf16[512,1024]{1,0:T(8,128)(2,1)} %k_hbm.1, bf16[512,1024]{1,0:T(8,128)(2,1)} %v_hbm.1, f32[8]{0:T(128)} %bias_hbm.1, s32[1,7]{1,0:T(1,128)} %src_hbm.1, s32[1,7]{1,0:T(1,128)} %blk_hbm.1, s32[1,7]{1,0:T(1,128)} %live_hbm.1), custom_call_target="tpu_custom_call" | custom-call | tf_op jit(solution)/shard_map/pallas_call | solution.py:675
  55.0 2.3 %copy.9 = bf16[512,1024]{1,0:T(8,128)(2,1)} copy(bf16[512,1024]{1,0:T(8,128)(2,1)} %shard_map.73) | data formatting | bytes 2097152

commit v3 on v2

--- a/solution.py
+++ b/solution.py
@@ -298,7 +298,8 @@
          6: ((7, 2, "prev"),),
          7: ((6, 3, "aux"),)}
 SLOTS = 6
-VMEM_LIMIT = 60 * 2 ** 20
+PARTS = 2
+VMEM_LIMIT = 40 * 2 ** 20
 
 
 def eight(list_len, heads, q_hbm, k_hbm, v_hbm, bias_hbm, src_hbm, blk_hbm, live_hbm, out_ref,
@@ -335,6 +336,75 @@
             want = jnp.where(hit, blk_ref[0, e], want)
         return want
 
+    pl.semaphore_wait(barrier, 7)
+
+    def remote(source, target, send, recv, device):
+        return pltpu.make_async_remote_copy(source, target, send, recv, device_id={"tm": device},
+                                            device_id_type=MESH)
+
+    def pieces(keys, values):
+        half = width // 2
+        return [part.at[:, pl.ds(i * half, half)] for i in range(2) for part in (keys, values)]
+
+    def prev_copy(i, keys, values, device):
+        return remote(pieces(keys, values)[i], pieces(prev_k, prev_v)[i], prev_ss.at[i], prev_rs.at[i], device)
+
+    def aux_copy(i, device):
+        return remote(pieces(k_hbm, v_hbm)[i], pieces(aux_k, aux_v)[i], aux_ss.at[i], aux_rs.at[i], device)
+
+    def list_copy(i, slot, device):
+        return remote(want_out, want_in.at[slot], list_ss.at[i], list_rs.at[slot], device)
+
+    def block_copies(slot, place, device):
+        wide = width // PARTS
+        return [remote(here.at[slot, :, pl.ds(j * wide, wide)], there.at[place, :, pl.ds(j * wide, wide)],
+                       blk_ss.at[i, j, slot], blk_rs.at[i, j, place], device)
+                for j in range(PARTS) for i, (here, there) in enumerate(((send_k, mem_k), (send_v, mem_v)))]
+
+    def pick(want, source, to_k, to_v):
+        from_k, from_v = {"own": (k_ref, v_ref), "prev": (prev_k, prev_v), "aux": (aux_k, aux_v)}[source]
+        ones = [jnp.where(want == b, 1.0, 0.0).astype(jnp.bfloat16) for b in range(per_seg)]
+
+        def one_strip(h, carry):
+            cols = pl.ds(pl.multiple_of(h * 128, 128), 128)
+            for origin, target in ((from_k, to_k), (from_v, to_v)):
+                total = origin[:BLOCK, cols] * ones[0]
+                for b in range(1, per_seg):
+                    total = total + origin[b * BLOCK:(b + 1) * BLOCK, cols] * ones[b]
+                target[:, cols] = total
+            return carry
+
+        lax.fori_loop(0, width // 128, one_strip, 0)
+
+    def pick_send(device, chosen):
+        for slot in chosen:
+            reader, distance, source = SENDS[device][slot]
+            pick(want_in[reader - 2, distance - 1:distance, :], source, send_k.at[slot], send_v.at[slot])
+
+    def start_send(device, chosen):
+        for slot in chosen:
+            reader, distance, source = SENDS[device][slot]
+            for c in block_copies(slot, ORDER[reader].index(distance), reader):
+                c.start()
+
+    def pick_own(place, source):
+        pick(jnp.full((1, 128), wants[place], jnp.int32), source, mem_k.at[place], mem_v.at[place])
+
+    def start_whole():
+        for i in range(4):
+            prev_copy(i, k_hbm, v_hbm, me + 1).start()
+
+    @pl.when(me == 3)
+    def _():
+        for i in range(4):
+            aux_copy(i, 7).start()
+
+    @pl.when(me == 0)
+    def _():
+        for i in range(4):
+            aux_copy(i, 4).start()
+    pl.when(any_of((0, 1, 2, 4, 6)))(start_whole)
+
     for load in loads[:3]:
         load.wait()
     wants = []
@@ -349,78 +419,13 @@
     for d in range(1, list_len + 1):
         tile = jnp.where(row == d - 1, want_of(d), tile)
     want_out[...] = tile
-    pl.semaphore_wait(barrier, 7)
-
-    def remote(source, target, send, recv, device):
-        return pltpu.make_async_remote_copy(source, target, send, recv, device_id={"tm": device},
-                                            device_id_type=MESH)
-
-    def pieces(keys, values):
-        half = width // 2
-        return [part.at[:, pl.ds(i * half, half)] for i in range(2) for part in (keys, values)]
-
-    def prev_copy(i, keys, values, device):
-        return remote(pieces(keys, values)[i], pieces(prev_k, prev_v)[i], prev_ss.at[i], prev_rs.at[i], device)
-
-    def aux_copy(i, device):
-        return remote(pieces(k_hbm, v_hbm)[i], pieces(aux_k, aux_v)[i], aux_ss.at[i], aux_rs.at[i], device)
-
-    def list_copy(i, slot, device):
-        return remote(want_out, want_in.at[slot], list_ss.at[i], list_rs.at[slot], device)
-
-    def block_copies(slot, place, device):
-        return [remote(here.at[slot], there.at[place], blk_ss.at[i, slot], blk_rs.at[i, place], device)
-                for i, (here, there) in enumerate(((send_k, mem_k), (send_v, mem_v)))]
-
-    def pick(want, source, to_k, to_v):
-        from_k, from_v = {"own": (k_ref, v_ref), "prev": (prev_k, prev_v), "aux": (aux_k, aux_v)}[source]
-        ones = [jnp.where(want == b, 1.0, 0.0).astype(jnp.bfloat16) for b in range(per_seg)]
-
-        def one_strip(h, carry):
-            cols = pl.ds(pl.multiple_of(h * 128, 128), 128)
-            for origin, target in ((from_k, to_k), (from_v, to_v)):
-                total = origin[:BLOCK, cols] * ones[0]
-                for b in range(1, per_seg):
-                    total = total + origin[b * BLOCK:(b + 1) * BLOCK, cols] * ones[b]
-                target[:, cols] = total
-            return carry
-
-        lax.fori_loop(0, width // 128, one_strip, 0)
-
-    def pick_send(device, chosen):
-        for slot in chosen:
-            reader, distance, source = SENDS[device][slot]
-            pick(want_in[reader - 2, distance - 1:distance, :], source, send_k.at[slot], send_v.at[slot])
-
-    def start_send(device, chosen):
-        for slot in chosen:
-            reader, distance, source = SENDS[device][slot]
-            for c in block_copies(slot, ORDER[reader].index(distance), reader):
-                c.start()
-
-    def pick_own(place, source):
-        pick(jnp.full((1, 128), wants[place], jnp.int32), source, mem_k.at[place], mem_v.at[place])
-
-    @pl.when(me == 3)
-    def _():
-        for i in range(4):
-            aux_copy(i, 7).start()
-
-    @pl.when(me == 0)
-    def _():
-        for i in range(4):
-            aux_copy(i, 4).start()
+
     for r in range(2, 8):
         @pl.when(me == r)
         def _():
             for i, holder in enumerate(HOLDERS[r]):
                 list_copy(i, r - 2, holder).start()
-    gives = any_of((0, 1, 2, 4, 5, 6))
-
-    @pl.when(gives)
-    def _():
-        for i in range(4):
-            prev_copy(i, k_hbm, v_hbm, me + 1).start()
+    pl.when(me == 5)(start_whole)
 
     for load in loads[3:]:
         load.wait()
@@ -441,7 +446,8 @@
             mem_k[place] = jnp.zeros((BLOCK, width), jnp.bfloat16)
             mem_v[place] = jnp.zeros((BLOCK, width), jnp.bfloat16)
 
-    def absorb(load_k, load_v, top, total, acc, some_wants=None, causal=False, first=False):
+    def absorb(load_k, load_v, top, total, acc, some_wants=None, causal=False, first=False,
+               span=None, close=None):
         lives = None if some_wants is None else [jnp.full((1, seg), w, jnp.int32) >= 0 for w in some_wants]
 
         def one_head(h, carry):
@@ -468,6 +474,10 @@
             part = jnp.sum(p, axis=0, keepdims=True)
             mixed = lax.dot_general(load_v(cols), p.astype(jnp.bfloat16), (((0,), (0,)), ((), ())),
                                     preferred_element_type=jnp.float32)
+            if close is not None:
+                shrink = jnp.exp2((top[row, :] - new) * slope)
+                close(h, total[row, :] * shrink + part, acc[cols, :] * shrink + mixed)
+                return carry
             if first:
                 total[row, :] = part
                 acc[cols, :] = mixed
@@ -478,7 +488,8 @@
             top[row, :] = new
             return carry
 
-        lax.fori_loop(0, heads, one_head, 0, unroll=UNROLL)
+        low, high = span or (0, heads)
+        lax.fori_loop(low, high, one_head, 0, unroll=min(UNROLL, high - low))
 
     @pl.when(me == 0)
     def _():
@@ -550,9 +561,8 @@
         for i in range(4):
             prev_copy(i, k_hbm, v_hbm, 2).wait_send()
         start_send(1, (2, 3))
-        for slot in (0, 1):
-            for c in block_copies(slot, 0, 2):
-                c.wait_send()
+        for c in block_copies(0, 0, 2) + block_copies(1, 0, 2)[:-1]:
+            c.wait_send()
         pl.semaphore_signal(turn, inc=1, device_id={"tm": 0}, device_id_type=MESH)
 
     @pl.when(me == 0)
@@ -574,42 +584,55 @@
         for reader, distance, source in entries:
             remote_places[reader].append(ORDER[reader].index(distance))
 
-    for low, count in STAGES:
-        for place in range(low, low + count):
-            readers = [r for r in range(8) if place in remote_places[r]]
-            if readers:
-                @pl.when(any_of(readers))
-                def _():
-                    for c in block_copies(0, place, 0):
-                        c.wait_recv()
-        users = [r for r in range(8) if any(ORDER[r][low:low + count])]
-
-        @pl.when(any_of(users))
-        def _():
-            def load(blocks):
-                return lambda c: blocks[low:low + count, :, c].reshape(count * BLOCK, hd)
-            absorb(load(mem_k), load(mem_v), top_m, sum_m, acc_m, some_wants=wants[low:low + count],
-                   first=low == 0)
-
-    def finish(h, carry):
+    def close(h, total, acc):
         cols = pl.ds(pl.multiple_of(h * hd, hd), hd)
         row = pl.ds(h, 1)
         gate = 1.0 / (1.0 + jnp.exp(jnp.full((1, seg), -bias_ref[h], jnp.float32)))
-        mixed = (acc_m[cols, :] * (gate / jnp.maximum(sum_m[row, :], 1.0))
+        mixed = (acc * (gate / jnp.maximum(total, 1.0))
                  + acc_l[cols, :] * ((1.0 - gate) / jnp.maximum(sum_l[row, :], 1.0)))
         out_ref[:, cols] = mixed.T.astype(jnp.bfloat16)
-        return carry
-
-    lax.fori_loop(0, heads, finish, 0, unroll=UNROLL)
+
+    def wait_blocks(place, chosen):
+        readers = [r for r in range(8) if place in remote_places[r]]
+        if readers:
+            @pl.when(any_of(readers))
+            def _():
+                for c in block_copies(0, place, 0)[chosen]:
+                    c.wait_recv()
+
+    last = len(STAGES) - 1
+    for stage, (low, count) in enumerate(STAGES):
+        users = [r for r in range(8) if any(ORDER[r][low:low + count])]
+
+        def load(blocks, low=low, count=count):
+            return lambda c: blocks[low:low + count, :, c].reshape(count * BLOCK, hd)
+
+        for part in range(PARTS if stage == last else 1):
+            for place in range(low, low + count):
+                wait_blocks(place, slice(2 * part, 2 * part + 2) if stage == last else slice(None))
+
+            @pl.when(any_of(users))
+            def _():
+                share = heads // PARTS
+                ending = dict(span=(part * share, part * share + share), close=close) if stage == last else {}
+                absorb(load(mem_k), load(mem_v), top_m, sum_m, acc_m, some_wants=wants[low:low + count],
+                       first=low == 0, **ending)
+
+    @pl.when(me <= 1)
+    def _():
+        def finish(h, carry):
+            close(h, sum_m[pl.ds(h, 1), :], acc_m[pl.ds(pl.multiple_of(h * hd, hd), hd), :])
+            return carry
+        lax.fori_loop(0, heads, finish, 0, unroll=UNROLL)
 
     for device in range(8):
         @pl.when(me == device)
         def _():
             for i in range(len(HOLDERS[device])):
                 list_copy(i, 0, 0).wait_send()
-            for slot in range(2 if device == 1 else 0, len(SENDS.get(device, ()))):
-                for c in block_copies(slot, 0, 0):
-                    c.wait_send()
+            sent = [c for slot in range(len(SENDS.get(device, ()))) for c in block_copies(slot, 0, 0)]
+            for c in sent[4 * PARTS - 1 if device == 1 else 0:]:
+                c.wait_send()
             if device in (0, 3):
                 for i in range(4):
                     aux_copy(i, 4).wait_send()
@@ -686,11 +709,11 @@
            pltpu.VMEM((width, seg), jnp.float32)] * 2
         + [pltpu.SemaphoreType.DMA((4,)), pltpu.SemaphoreType.DMA((6,))]
         + [pltpu.SemaphoreType.DMA((4,))] * 4
-        + [pltpu.SemaphoreType.DMA((2, SLOTS)), pltpu.SemaphoreType.DMA((2, len(ORDER[0]))),
+        + [pltpu.SemaphoreType.DMA((2, PARTS, SLOTS)), pltpu.SemaphoreType.DMA((2, PARTS, len(ORDER[0]))),
            pltpu.SemaphoreType.REGULAR],
         compiler_params=pltpu.CompilerParams(collective_id=0, has_side_effects=True,
                                              vmem_limit_bytes=VMEM_LIMIT),
-    )(q_proj, k_proj, v_proj, gate_bias, src_shard, src_block, valid)
+    )(*[pltpu.with_memory_space_constraint(x, pltpu.HBM) for x in (q_proj, k_proj, v_proj, gate_bias, src_shard, src_block, valid)])
 
 
 def solution(mesh):

time: 57.4 us -> 53 us (0.923)
  the two profiles are of different devices: /device:TPU:27 before, /device:TPU:15 now
where the time goes in v3:
time: 53 us; the launch traced here: 52 us
  Pallas kernels  51 us (96%)
  local copies, waits for them, and re-layouts  0.97 us (2%)
    pallas_call x1, Pallas kernels, shards(): pl.pallas_call(functools.partial(eight, list_len, heads), out_shape=jax.S...  51 us

profile of v3, /device:TPU:15, one launch (start us, length us, event | category | flops | bytes accessed | tf_op | source)
XLA Modules:
  0.0 52.0 jit_solution(14018027042586758532)
XLA Ops:
  0.0 51.0 %shard_map.73 = bf16[512,1024]{1,0:T(8,128)(2,1)S(1)} custom-call(bf16[512,1024]{1,0:T(8,128)(2,1)} %q_hbm.1, bf16[512,1024]{1,0:T(8,128)(2,1)} %k_hbm.1, bf16[512,1024]{1,0:T(8,128)(2,1)} %v_hbm.1, f32[8]{0:T(128)} %bias_hbm.1, s32[1,7]{1,0:T(1,128)} %src_hbm.1, s32[1,7]{1,0:T(1,128)} %blk_hbm.1, s32[1,7]{1,0:T(1,128)} %live_hbm.1), custom_call_target="tpu_custom_call" | custom-call | tf_op jit(solution)/shard_map/pallas_call | solution.py:698
  51.0 1.0 %copy.9 = bf16[512,1024]{1,0:T(8,128)(2,1)} copy(bf16[512,1024]{1,0:T(8,128)(2,1)S(1)} %shard_map.73) | data formatting | bytes 2097152

commit v4 on v3

--- a/solution.py
+++ b/solution.py
@@ -305,7 +305,7 @@
 def eight(list_len, heads, q_hbm, k_hbm, v_hbm, bias_hbm, src_hbm, blk_hbm, live_hbm, out_ref,
           q_ref, k_ref, v_ref, bias_ref, src_ref, blk_ref, live_ref, load_s, prev_k, prev_v, aux_k, aux_v, mem_k, mem_v, send_k, send_v, want_out, want_in,
           top_l, sum_l, acc_l, top_m, sum_m, acc_m,
-          list_ss, list_rs, prev_ss, prev_rs, aux_ss, aux_rs, blk_ss, blk_rs, turn):
+          list_ss, list_rs, prev_ss, prev_rs, aux_ss, aux_rs, blk_ss, blk_rs, turn, here):
     me = lax.axis_index("tm")
     seg, width = q_ref.shape
     hd = width // heads
@@ -315,11 +315,16 @@
          (k_hbm, k_ref), (q_hbm, q_ref), (v_hbm, v_ref)))]
     for load in loads:
         load.start()
+    chip, core = me // 2, me % 2
+    beside = [chip * 2 + 1 - core] + [other * 2 + i for other in (chip + 1 - 2 * (chip % 2), (chip + 2) % 4)
+                                      for i in range(2)]
+
+    def greet(semaphore):
+        for other in beside:
+            pl.semaphore_signal(semaphore, inc=1, device_id={"tm": other}, device_id_type=MESH)
+
     barrier = pltpu.get_barrier_semaphore()
-    for other in range(8):
-        @pl.when(me != other)
-        def _():
-            pl.semaphore_signal(barrier, inc=1, device_id={"tm": other}, device_id_type=MESH)
+    greet(barrier)
     places = len(ORDER[0])
     slope = math.log2(math.e) / math.sqrt(hd)
 
@@ -336,7 +341,8 @@
             want = jnp.where(hit, blk_ref[0, e], want)
         return want
 
-    pl.semaphore_wait(barrier, 7)
+    pl.semaphore_wait(barrier, len(beside))
+    greet(here)
 
     def remote(source, target, send, recv, device):
         return pltpu.make_async_remote_copy(source, target, send, recv, device_id={"tm": device},
@@ -357,9 +363,9 @@
 
     def block_copies(slot, place, device):
         wide = width // PARTS
-        return [remote(here.at[slot, :, pl.ds(j * wide, wide)], there.at[place, :, pl.ds(j * wide, wide)],
+        return [remote(origin.at[slot, :, pl.ds(j * wide, wide)], target.at[place, :, pl.ds(j * wide, wide)],
                        blk_ss.at[i, j, slot], blk_rs.at[i, j, place], device)
-                for j in range(PARTS) for i, (here, there) in enumerate(((send_k, mem_k), (send_v, mem_v)))]
+                for j in range(PARTS) for i, (origin, target) in enumerate(((send_k, mem_k), (send_v, mem_v)))]
 
     def pick(want, source, to_k, to_v):
         from_k, from_v = {"own": (k_ref, v_ref), "prev": (prev_k, prev_v), "aux": (aux_k, aux_v)}[source]
@@ -404,6 +410,10 @@
         for i in range(4):
             aux_copy(i, 4).start()
     pl.when(any_of((0, 1, 2, 4, 6)))(start_whole)
+
+    @pl.when(me == 5)
+    def _():
+        prev_copy(0, k_hbm, v_hbm, me + 1).start()
 
     for load in loads[:3]:
         load.wait()
@@ -420,12 +430,17 @@
         tile = jnp.where(row == d - 1, want_of(d), tile)
     want_out[...] = tile
 
+    pl.semaphore_wait(here, len(beside))
     for r in range(2, 8):
         @pl.when(me == r)
         def _():
             for i, holder in enumerate(HOLDERS[r]):
                 list_copy(i, r - 2, holder).start()
-    pl.when(me == 5)(start_whole)
+
+    @pl.when(me == 5)
+    def _():
+        for i in range(1, 4):
+            prev_copy(i, k_hbm, v_hbm, me + 1).start()
 
     for load in loads[3:]:
         load.wait()
@@ -710,7 +725,7 @@
         + [pltpu.SemaphoreType.DMA((4,)), pltpu.SemaphoreType.DMA((6,))]
         + [pltpu.SemaphoreType.DMA((4,))] * 4
         + [pltpu.SemaphoreType.DMA((2, PARTS, SLOTS)), pltpu.SemaphoreType.DMA((2, PARTS, len(ORDER[0]))),
-           pltpu.SemaphoreType.REGULAR],
+           pltpu.SemaphoreType.REGULAR, pltpu.SemaphoreType.REGULAR],
         compiler_params=pltpu.CompilerParams(collective_id=0, has_side_effects=True,
                                              vmem_limit_bytes=VMEM_LIMIT),
     )(*[pltpu.with_memory_space_constraint(x, pltpu.HBM) for x in (q_proj, k_proj, v_proj, gate_bias, src_shard, src_block, valid)])

time: 53 us -> 52.1 us (0.983); the launches traced: 52 us -> 51.7 us
  no operation moved by 1% of the time
where the time goes in v4:
time: 52.1 us; the launch traced here: 51.7 us
  Pallas kernels  50.7 us (97%)
  local copies, waits for them, and re-layouts  0.97 us (2%)
    pallas_call x1, Pallas kernels, shards(): pl.pallas_call(functools.partial(eight, list_len, heads), out_shape=jax.S...  50.7 us

profile of v4, /device:TPU:15, one launch (start us, length us, event | category | flops | bytes accessed | tf_op | source)
XLA Modules:
  0.0 51.7 jit_solution(8138593219330712489)
XLA Ops:
  0.0 50.7 %shard_map.73 = bf16[512,1024]{1,0:T(8,128)(2,1)S(1)} custom-call(bf16[512,1024]{1,0:T(8,128)(2,1)} %q_hbm.1, bf16[512,1024]{1,0:T(8,128)(2,1)} %k_hbm.1, bf16[512,1024]{1,0:T(8,128)(2,1)} %v_hbm.1, f32[8]{0:T(128)} %bias_hbm.1, s32[1,7]{1,0:T(1,128)} %src_hbm.1, s32[1,7]{1,0:T(1,128)} %blk_hbm.1, s32[1,7]{1,0:T(1,128)} %live_hbm.1), custom_call_target="tpu_custom_call" | custom-call | tf_op jit(solution)/shard_map/pallas_call | solution.py:713
  50.7 1.0 %copy.9 = bf16[512,1024]{1,0:T(8,128)(2,1)} copy(bf16[512,1024]{1,0:T(8,128)(2,1)S(1)} %shard_map.73) | data formatting | bytes 2097152
